TPU v7x, 128 devices: a whole 4x4x4 slice. The times are simulated.
128 devices in a mesh: gx: 16 (over z, y_lo, core), gy: 8 (over x, y_hi).
Axes of the slice: x: 4, y: 4 (y_hi: 2, y_lo: 2; y = y_hi * 2 + y_lo), z: 4, core: 2. Of those that a mesh axis runs over, the one named last changes fastest.
Arguments:
- velocity: float32 [3, 4096, 1024], P(None, 'gx', 'gy'), may hold values from 0.4 to 1.6
- adjoint_seed: float32 [3, 4096, 1024], P(None, 'gx', 'gy'), may hold values from -6 to 6
- courant: float32 [3, 4096, 1024], P(None, 'gx', 'gy'), may hold values from 0.1 to 0.45
- viscosity: float32 [3, 4096, 1024], P(None, 'gx', 'gy'), may hold values from 0.02 to 0.1
- turbine_tile: int32 [512, 1], P(('gx', 'gy')), may hold values from 0 to 127; in each aligned block of 512 rows (0 to 511, 512 to 1023, ...) at most 12 rows name the same one
- turbine_offset: int32 [512, 2], P(('gx', 'gy')), may hold values from 0 to 64
- thrust: float32 [512], P(('gx', 'gy')), may hold values from 0.5 to 2
- disk_width: float32 [512], P(('gx', 'gy')), may hold values from 8 to 16
Outputs:
- adjoint_start: float32 [3, 4096, 1024], P(None, 'gx', 'gy')
- thrust_grad: float32 [512], P(('gx', 'gy'))
Inputs may be any that keep to these rules, and one draw needn't show every extreme that they name: `turbine_tile`: each turbine's tile is the index along gx times the number of devices of gy plus the index along gy of the device whose cells hold its footprint. No tile holds more than 12 turbines, and some tile holds exactly 12.
All inputs are finite; a program needn't handle non-finite values.
Results may differ from a plain program's by a relative error of at most 0.00002.
Values sent between devices are 32-bit elements; how exact they have to be, the bound alone decides.
A program may use at most 128 MiB of HBM per device.

v0:
```python
import jax
import jax.numpy as jnp
from jax import lax
from jax.sharding import PartitionSpec as P

LEV = 3
STEPS = 8
FP = 64


VERTICAL_MIX = 0.05
DRAG_SCALE = 0.01


def padded_2(block, sides, width):
    for axis, dim in sides:
        count = lax.axis_size(axis)
        forward = [(i, i + 1) for i in range(count - 1)]
        forward.append((count - 1, 0))
        backward = [(target, source) for source, target in forward]
        low = lax.ppermute(
            lax.slice_in_dim(block, block.shape[dim] - width, None, axis=dim), axis, forward
        )
        high = lax.ppermute(lax.slice_in_dim(block, 0, width, axis=dim), axis, backward)
        block = jnp.concatenate([low, block, high], axis=dim)
    return block


def drag_law(state):
    return state * jnp.sqrt(state * state + 1.0)


def drag_slope(state):
    square_one = state * state + 1.0
    return (square_one + state * state) / jnp.sqrt(square_one)


def vertical(center):
    zero_row = jnp.zeros_like(center[:1])
    from_above = jnp.concatenate([center[1:] - center[:-1], zero_row], axis=0)
    from_below = jnp.concatenate([zero_row, center[:-1] - center[1:]], axis=0)
    return from_above + from_below


def advance(padded, advect, diffuse, drag_coef):
    center = padded[:, 1:-1, 1:-1]
    upwind = padded[:, :-2, 1:-1]
    downwind = padded[:, 2:, 1:-1]
    left_cell = padded[:, 1:-1, :-2]
    right_cell = padded[:, 1:-1, 2:]
    return (
        center
        + advect * (upwind - center)
        + diffuse * (downwind + upwind + right_cell + left_cell - 4.0 * center)
        + VERTICAL_MIX * vertical(center)
        - drag_coef * drag_law(center)
    )


def retreat(padded, advect_ext, diffuse_ext, drag_coef, state):
    flux_adv = advect_ext * padded
    flux_dif = diffuse_ext * padded
    center = padded[:, 1:-1, 1:-1]
    return (
        center
        - flux_adv[:, 1:-1, 1:-1]
        - 4.0 * flux_dif[:, 1:-1, 1:-1]
        + flux_adv[:, 2:, 1:-1]
        + (
            flux_dif[:, 2:, 1:-1]
            + flux_dif[:, :-2, 1:-1]
            + flux_dif[:, 1:-1, 2:]
            + flux_dif[:, 1:-1, :-2]
        )
        + VERTICAL_MIX * vertical(center)
        - drag_coef * drag_slope(state) * center
    )


def footprint(disk_width):
    cell_pos = jnp.arange(FP, dtype=jnp.float32) - (FP - 1) / 2.0
    profile = jnp.exp(
        -(cell_pos[None, :] * cell_pos[None, :]) / (2.0 * disk_width[:, None] * disk_width[:, None])
    )
    level_pos = jnp.arange(LEV, dtype=jnp.float32) - (LEV - 1) / 2.0
    level_gain = DRAG_SCALE * jnp.exp(-0.5 * level_pos * level_pos)
    return level_gain[None, :, None, None] * profile[:, None, :, None] * profile[:, None, None, :]


def extend_rim(array, rim_depth):
    return padded_2(array, (("gx", 1), ("gy", 2)), rim_depth)


def trim_rim(array, stored_margin, wanted):
    excess = stored_margin - wanted
    if excess == 0:
        return array
    return array[:, excess:-excess, excess:-excess]


def coef_at(coef_ext, coef_margin, wanted, levels):
    portion = trim_rim(coef_ext, coef_margin, wanted)
    return (portion[:levels], portion[levels : 2 * levels], portion[2 * levels : 3 * levels])


def shards(
    velocity, adjoint_seed, courant, viscosity, turbine_tile, turbine_offset, thrust, disk_width
):
    levels = velocity.shape[0]
    places, shifts = (
        lax.all_gather(turbine_tile, ("gx", "gy"), axis=0, tiled=True),
        lax.all_gather(turbine_offset, ("gx", "gy"), axis=0, tiled=True),
    )
    thrusts, widths = (
        lax.all_gather(thrust, ("gx", "gy"), axis=0, tiled=True),
        lax.all_gather(disk_width, ("gx", "gy"), axis=0, tiled=True),
    )
    turbine_count = places.shape[0]
    own_index = lax.axis_index("gx") * lax.axis_size("gy") + lax.axis_index("gy")
    turbine_ids = jnp.arange(turbine_count, dtype=jnp.int32)
    in_tile = places[:, 0] == own_index
    sort_keys = jnp.where(in_tile, turbine_ids, turbine_ids + turbine_count)
    slot_count = 3 * thrust.shape[0]
    slot_ids = jnp.argsort(sort_keys)[:slot_count]
    slot_match = in_tile[slot_ids]
    slot_live = slot_match.astype(jnp.float32)
    slot_rows = shifts[slot_ids, 0]
    slot_cols = shifts[slot_ids, 1]
    kernels = footprint(widths[slot_ids])
    slot_thrust = thrusts[slot_ids] * slot_live

    def add_turbine(slot_index, field_now):
        corner = (jnp.int32(0), slot_rows[slot_index], slot_cols[slot_index])
        block_vals = lax.dynamic_slice(field_now, corner, (levels, FP, FP))
        return lax.dynamic_update_slice(
            field_now, block_vals + slot_thrust[slot_index] * kernels[slot_index], corner
        )

    drag_field = lax.fori_loop(0, slot_count, add_turbine, jnp.zeros_like(velocity))
    forward_depth = 1
    coef_margin = 1
    coef_margin = forward_depth
    coef_ext = extend_rim(jnp.concatenate([courant, viscosity, drag_field], axis=0), forward_depth)
    state = velocity
    state_margin = 0
    states = []
    for step_index in range(STEPS):
        if step_index + 1 < STEPS and state_margin == 0:
            state = extend_rim(state, forward_depth)
            state_margin = forward_depth
        states.append((state, state_margin))
        if step_index + 1 < STEPS:
            advect, diffuse, drag_coef = coef_at(coef_ext, coef_margin, state_margin - 1, levels)
            state = advance(state, advect, diffuse, drag_coef)
            state_margin = state_margin - 1
    adjoint = adjoint_seed
    adjoint_margin = 0
    sensitivity = jnp.zeros_like(velocity)
    for step_index in reversed(range(STEPS)):
        stored, stored_margin = states[step_index]
        sensitivity = sensitivity - trim_rim(adjoint, adjoint_margin, 0) * drag_law(
            trim_rim(stored, stored_margin, 0)
        )
        adjoint = extend_rim(adjoint, forward_depth)
        adjoint_margin = forward_depth
        advect_ext, diffuse_ext, unused_drag = coef_at(
            coef_ext, coef_margin, adjoint_margin, levels
        )
        unused_adv, unused_dif, drag_mid = coef_at(
            coef_ext, coef_margin, adjoint_margin - 1, levels
        )
        adjoint = retreat(
            adjoint,
            advect_ext,
            diffuse_ext,
            drag_mid,
            trim_rim(stored, stored_margin, adjoint_margin - 1),
        )
        adjoint_margin = adjoint_margin - 1
    adjoint_start = trim_rim(adjoint, adjoint_margin, 0)

    def slot_total(row_first, col_first, kernel):
        block_vals = lax.dynamic_slice(
            sensitivity, (jnp.int32(0), row_first, col_first), (levels, FP, FP)
        )
        return jnp.sum(kernel * block_vals)

    totals = jax.vmap(slot_total)(slot_rows, slot_cols, kernels)
    values = thrusts[slot_ids] * totals * slot_live
    one_hot = (turbine_ids[None, :] == slot_ids[:, None]).astype(jnp.float32)
    spread = jnp.sum(one_hot * values[:, None], axis=0)
    return (adjoint_start, lax.psum_scatter(spread, ("gx", "gy"), scatter_dimension=0, tiled=True))


def solution(mesh):
    placed = (
        P(None, "gx", "gy"),
        P(None, "gx", "gy"),
        P(None, "gx", "gy"),
        P(None, "gx", "gy"),
        P(("gx", "gy"), None),
        P(("gx", "gy"), None),
        P(("gx", "gy")),
        P(("gx", "gy")),
    )
    return jax.shard_map(
        shards,
        mesh=mesh,
        in_specs=placed,
        out_specs=(P(None, "gx", "gy"), P(("gx", "gy"))),
        check_vma=False,
    )
```

profile of v0, /device:TPU:1, one launch (start us, length us, event | category | flops | bytes accessed | tf_op | source)
XLA Modules:
  0.0 1061.2 jit_solution(10426289407377339527)
XLA Ops:
  6.1 69.8 %all-reduce.32 = s32[512]{0:T(512)S(1)} all-reduce(s32[512]{0:T(512)S(1)} %bitcast_dynamic-update-slice_fusion.1), channel_id=1, replica_groups=mesh['gx'=16,'gy'=8] {'gx','gy'}, use_global_device_ids=true, to_apply=%add.32 | all-reduce | flops 512 | bytes 4096
  75.9 3.8 sort.17
  80.3 303.1 %all-gather = s32[128,4,2]{1,2,0:T(2,128)S(1)} all-gather(s32[1,4,2]{1,2,0:T(2,128)} %bitcast.32), channel_id=1, replica_groups=mesh['gx'=16,'gy'=8] {'gx','gy'}, dimensions={0}, use_global_device_ids=true | all-gather | bytes 4128 | tf_op jit(solution)/shard_map/all_gather | solution.py:112
  386.2 71.6 %all-reduce.36 = (f32[512]{0:T(512)S(1)}, f32[512]{0:T(512)S(1)}) all-reduce(f32[512]{0:T(512)S(1)} %dynamic-update-slice.3, f32[512]{0:T(512)S(1)} %dynamic-update-slice.4), channel_id=1, replica_groups=mesh['gx'=16,'gy'=8] {'gx','gy'}, use_global_device_ids=true, to_apply=%add.33 | all-reduce | flops 1024 | bytes 8192
  460.0 99.8 %while.14 = (s32[]{:T(128)}, f32[3,256,128]{2,1,0:T(8,128)S(1)}, s32[12]{0:T(128)S(1)}, s32[12]{0:T(128)S(1)}, f32[12]{0:T(128)S(1)}, /*index=5*/f32[12,3,64,64]...) while((s32[]{:T(128)}, f32[3,256,128]{2,1,0:T(8,128)S(1)}, s32[12]{0:T(128)S(1)}, ...), condition=%wide.region_2.3_spmd, body=%wide.region_1.2_spmd.sunk | while | flops 24584 | bytes 245993 | solution.py:139
  563.2 3.6 collective-permute-start.10
  569.3 3.4 fusion.4
  579.1 3.5 collective-permute-start.14
  584.9 6.0 fusion.113
  591.0 4.8 collective-permute-start.17
  602.0 5.0 collective-permute-start.18
  609.3 5.9 fusion.102
  615.3 3.0 collective-permute-start.21
  624.7 2.7 collective-permute-start.23
  627.7 2.9 collective-permute-start.22
  632.9 5.9 fusion.91
  638.9 5.9 collective-permute-start.25
  645.2 4.7 collective-permute-start.7
  653.1 5.1 collective-permute-start.26
  660.6 6.0 fusion.80
  674.3 5.0 collective-permute-start.30
  682.4 5.0 fusion.69
  687.4 3.3 collective-permute-start.33
  699.8 3.9 collective-permute-start.34
  704.3 2.7 fusion.150
  707.0 2.6 copy.630
  709.6 2.6 collective-permute-start.3
  712.2 2.6 copy.629
  719.9 2.6 copy.632
  722.5 2.6 copy.631
  725.1 5.1 fusion.131
  730.4 4.9 fusion.130
  735.5 4.1 fusion.121
  739.6 5.7 collective-permute-start.37
  751.4 4.7 collective-permute-start.39
  762.4 2.3 collective-permute-done.38
  766.6 2.5 fusion.147
  770.8 6.0 collective-permute-start.41
  794.0 2.5 fusion.145
  798.2 5.3 collective-permute-start.45
  820.9 2.5 fusion.143
  825.1 5.3 collective-permute-start.49
  847.7 2.5 fusion.141
  852.0 5.3 collective-permute-start.53
  874.7 2.5 fusion.139
  880.4 5.3 collective-permute-start.57
  896.4 2.3 slice_subtract_fusion.11
  903.6 2.5 fusion.137
  906.6 9.2 multiply_subtract_fusion
  916.8 5.4 collective-permute-start.61
  923.2 49.5 %while.15 = (s32[]{:T(128)}, f32[3,256,128]{2,1,0:T(8,128)}, s32[12,3]{0,1:T(4,128)}, f32[12,3,64,64]{3,2,1,0:T(8,128)}, s32[]{:T(128)}) while((s32[]{:T(128)}, f32[3,256,128]{2,1,0:T(8,128)}, s32[12,3]{0,1:T(4,128)}, f32[12,3,64,64]{3,2,1,0:T(8,128)}, s32[]{:T(128)}) %tuple.129), condition=%wide.while_cond, body=%wide.while_body.sunk | while | flops 2 | bytes 197749 | solution.py:183
  924.6 2.8 bitcast_dynamic-update-slice_fusion.3
  928.7 2.8 bitcast_dynamic-update-slice_fusion.3
  932.8 2.8 bitcast_dynamic-update-slice_fusion.3
  936.9 2.8 bitcast_dynamic-update-slice_fusion.3
  941.0 2.8 bitcast_dynamic-update-slice_fusion.3
  945.2 2.8 bitcast_dynamic-update-slice_fusion.3
  949.3 2.8 bitcast_dynamic-update-slice_fusion.3
  953.4 2.8 bitcast_dynamic-update-slice_fusion.3
  957.6 2.8 bitcast_dynamic-update-slice_fusion.3
  961.7 2.8 bitcast_dynamic-update-slice_fusion.3
  965.8 2.8 bitcast_dynamic-update-slice_fusion.3
  969.9 2.8 bitcast_dynamic-update-slice_fusion.3
  985.3 65.9 %all-reduce.35 = f32[512]{0:T(512)} all-reduce(f32[512]{0:T(512)} %select_reduce_fusion), channel_id=2, replica_groups=mesh['gx'=16,'gy'=8] {'gx','gy'}, use_global_device_ids=true, to_apply=%region_5.6.clone | all-reduce | flops 512 | bytes 4096
  (570 shorter events, 276.0 us)
Async XLA Ops:
  1.4 559.4 %collective-permute-start.9 = (f32[3,1,128]{2,1,0:T(1,128)S(1)}, f32[3,1,128]{2,1,0:T(1,128)S(1)}, u32[]{:S(2)}, u32[]{:S(2)}) collective-permute-start(f32[3,1,128]{2,1,0:T(1,128)S(1)} %get-tuple-element.326), channel_id=1, source_target_pairs={{8,0},{16,8},{24,16},{32,24},{40,32},{48,40},{56,48},{64,56},{72,6... | collective-permute-start | bytes 4616 | tf_op jit(solution)/shard_map/ppermute | solution.py:24
  2.8 558.0 %collective-permute-start.8 = (f32[3,1,128]{2,1,0:T(1,128)S(1)}, f32[3,1,128]{2,1,0:T(1,128)S(1)}, u32[]{:S(2)}, u32[]{:S(2)}) collective-permute-start(f32[3,1,128]{2,1,0:T(1,128)S(1)} %get-tuple-element.327), channel_id=1, source_target_pairs={{0,8},{8,16},{16,24},{24,32},{32,40},{40,48},{48,56},{56,64},{64,7... | collective-permute-start | bytes 4616 | tf_op jit(solution)/shard_map/ppermute | solution.py:21
  561.4 6.5 collective-permute-start.11
  563.2 5.0 collective-permute-start.10
  572.8 3.1 collective-permute-start.13
  574.7 1.3 collective-permute-start.12
  576.9 6.6 collective-permute-start.15
  579.1 4.7 collective-permute-start.14
  591.0 7.7 collective-permute-start.17
  595.8 2.9 collective-permute-start.16
  595.8 22.9 %collective-permute-start.5 = (f32[3,1,128]{2,1,0:T(1,128)S(1)}, f32[3,1,128]{2,1,0:T(1,128)S(1)}, u32[]{:S(2)}, u32[]{:S(2)}) collective-permute-start(f32[3,1,128]{2,1,0:T(1,128)S(1)} %get-tuple-element.329), channel_id=1, source_target_pairs={{8,0},{16,8},{24,16},{32,24},{40,32},{48,40},{56,48},{64,56},{72,6... | collective-permute-start | bytes 4616 | tf_op jit(solution)/shard_map/ppermute | solution.py:24
  596.4 22.9 %collective-permute-start.4 = (f32[3,1,128]{2,1,0:T(1,128)S(1)}, f32[3,1,128]{2,1,0:T(1,128)}, u32[]{:S(2)}, u32[]{:S(2)}) collective-permute-start(f32[3,1,128]{2,1,0:T(1,128)S(1)} %get-tuple-element.328), channel_id=1, source_target_pairs={{0,8},{8,16},{16,24},{24,32},{32,40},{40,48},{48,56},{56,64},{64,7... | collective-permute-start | bytes 4616 | tf_op jit(solution)/shard_map/ppermute | solution.py:21
  601.3 6.6 collective-permute-start.19
  602.0 6.3 collective-permute-start.18
  615.3 4.7 collective-permute-start.21
  618.3 3.8 collective-permute-start.20
  624.7 6.7 collective-permute-start.23
  627.7 4.1 collective-permute-start.22
  638.9 11.3 %collective-permute-start.25 = (f32[3,1,128]{2,0,1:T(4,128)S(1)}, f32[3,1,128]{2,0,1:T(4,128)S(1)}, u32[]{:S(2)}, u32[]{:S(2)}) collective-permute-start(f32[3,1,128]{2,0,1:T(4,128)S(1)} %get-tuple-element.299), channel_id=1, source_target_pairs={{8,0},{16,8},{24,16},{32,24},{40,32},{48,40},{56,48},{64,56},{72,6... | collective-permute-start | bytes 4616 | tf_op jit(solution)/shard_map/ppermute | solution.py:24
  644.7 5.5 collective-permute-start.24
  645.2 25.3 %collective-permute-start.7 = (f32[3,258,1]{1,0,2:T(4,128)S(1)}, f32[3,258,1]{1,0,2:T(4,128)S(1)}, u32[]{:S(2)}, u32[]{:S(2)}) collective-permute-start(f32[3,258,1]{1,0,2:T(4,128)S(1)} %copy.743), channel_id=1, source_target_pairs={{1,0},{2,1},{3,2},{4,3},{5,4},{6,5},{7,6},{0,7},{9,8},{10,9},{11,1... | collective-permute-start | bytes 9296 | tf_op jit(solution)/shard_map/ppermute | solution.py:24
  650.2 21.5 %collective-permute-start.6 = (f32[3,258,1]{1,0,2:T(4,128)S(1)}, f32[3,258,1]{1,0,2:T(4,128)S(1)}, u32[]{:S(2)}, u32[]{:S(2)}) collective-permute-start(f32[3,258,1]{1,0,2:T(4,128)S(1)} %copy.742), channel_id=1, source_target_pairs={{0,1},{1,2},{2,3},{3,4},{4,5},{5,6},{6,7},{7,0},{8,9},{9,10},{10,1... | collective-permute-start | bytes 9296 | tf_op jit(solution)/shard_map/ppermute | solution.py:21
  652.8 6.3 collective-permute-start.27
  653.1 6.3 collective-permute-start.26
  666.6 6.2 collective-permute-start.29
  668.4 4.4 collective-permute-start.28
  673.6 6.6 collective-permute-start.31
  674.3 7.0 collective-permute-start.30
  687.4 5.3 collective-permute-start.33
  690.7 2.5 collective-permute-start.32
  690.8 12.9 %collective-permute-start.1 = (f32[9,1,128]{2,0,1:T(8,128)S(1)}, f32[9,1,128]{2,0,1:T(8,128)S(1)}, u32[]{:S(2)}, u32[]{:S(2)}) collective-permute-start(f32[9,1,128]{2,0,1:T(8,128)S(1)} %get-tuple-element.233), channel_id=1, source_target_pairs={{8,0},{16,8},{24,16},{32,24},{40,32},{48,40},{56,48},{64,56},{72,6... | collective-permute-start | bytes 13832 | tf_op jit(solution)/shard_map/ppermute | solution.py:24
  692.7 11.0 %collective-permute-start = (f32[9,1,128]{2,0,1:T(8,128)S(1)}, f32[9,1,128]{2,0,1:T(8,128)S(1)}, u32[]{:S(2)}, u32[]{:S(2)}) collective-permute-start(f32[9,1,128]{2,0,1:T(8,128)S(1)} %get-tuple-element.232), channel_id=1, source_target_pairs={{0,8},{8,16},{16,24},{24,32},{32,40},{40,48},{48,56},{56,64},{64,7... | collective-permute-start | bytes 13832 | tf_op jit(solution)/shard_map/ppermute | solution.py:21
  696.7 19.7 %collective-permute-start.35 = (f32[3,258,1]{1,0,2:T(4,128)S(1)}, f32[3,258,1]{1,0,2:T(4,128)}, u32[]{:S(2)}, u32[]{:S(2)}) collective-permute-start(f32[3,258,1]{1,0,2:T(4,128)S(1)} %copy.698), channel_id=1, source_target_pairs={{0,1},{1,2},{2,3},{3,4},{4,5},{5,6},{6,7},{7,0},{8,9},{9,10},{10,1... | collective-permute-start | bytes 9296 | tf_op jit(solution)/shard_map/ppermute | solution.py:21
  699.8 18.3 %collective-permute-start.34 = (f32[3,258,1]{1,0,2:T(4,128)}, f32[3,258,1]{1,0,2:T(4,128)}, u32[]{:S(2)}, u32[]{:S(2)}) collective-permute-start(f32[3,258,1]{1,0,2:T(4,128)} %copy.696), channel_id=1, source_target_pairs={{1,0},{2,1},{3,2},{4,3},{5,4},{6,5},{7,6},{0,7},{9,8},{10,9},{11,1... | collective-permute-start | bytes 9296 | tf_op jit(solution)/shard_map/ppermute | solution.py:24
  709.6 10.4 collective-permute-start.3
  714.8 7.7 collective-permute-start.2
  739.6 6.5 collective-permute-start.37
  745.2 2.2 collective-permute-start.36
  751.4 9.3 collective-permute-start.39
  758.0 6.8 collective-permute-start.38
  770.8 6.8 collective-permute-start.41
  776.8 1.2 collective-permute-start.40
  782.0 7.1 collective-permute-start.43
  785.8 6.4 collective-permute-start.42
  798.2 6.2 collective-permute-start.45
  803.6 1.2 collective-permute-start.44
  808.8 7.3 collective-permute-start.47
  812.5 6.6 collective-permute-start.46
  825.1 6.2 collective-permute-start.49
  830.5 1.2 collective-permute-start.48
  835.7 7.1 collective-permute-start.51
  839.5 6.4 collective-permute-start.50
  852.0 6.2 collective-permute-start.53
  857.3 1.2 collective-permute-start.52
  862.6 7.3 collective-permute-start.55
  866.3 6.6 collective-permute-start.54
  880.4 6.4 collective-permute-start.57
  885.6 1.5 collective-permute-start.56
  891.5 7.2 collective-permute-start.59
  895.3 6.4 collective-permute-start.58
  916.8 58.3 %collective-permute-start.61 = (f32[3,1,128]{2,0,1:T(4,128)}, f32[3,1,128]{2,0,1:T(4,128)}, u32[]{:S(2)}, u32[]{:S(2)}) collective-permute-start(f32[3,1,128]{2,0,1:T(4,128)} %get-tuple-element.263), channel_id=1, source_target_pairs={{8,0},{16,8},{24,16},{32,24},{40,32},{48,40},{56,48},{64,56},{72,6... | collective-permute-start | bytes 4616 | tf_op jit(solution)/shard_map/ppermute | solution.py:24
  922.2 52.9 %collective-permute-start.60 = (f32[3,1,128]{2,0,1:T(4,128)}, f32[3,1,128]{2,0,1:T(4,128)}, u32[]{:S(2)}, u32[]{:S(2)}) collective-permute-start(f32[3,1,128]{2,0,1:T(4,128)} %get-tuple-element.262), channel_id=1, source_target_pairs={{0,8},{8,16},{16,24},{24,32},{32,40},{40,48},{48,56},{56,64},{64,7... | collective-permute-start | bytes 4616 | tf_op jit(solution)/shard_map/ppermute | solution.py:21
  979.1 73.3 %collective-permute-start.63 = (f32[3,258,1]{1,0,2:T(4,128)}, f32[3,258,1]{1,0,2:T(4,128)}, u32[]{:S(2)}, u32[]{:S(2)}) collective-permute-start(f32[3,258,1]{1,0,2:T(4,128)} %copy.735), channel_id=1, source_target_pairs={{1,0},{2,1},{3,2},{4,3},{5,4},{6,5},{7,6},{0,7},{9,8},{10,9},{11,1... | collective-permute-start | bytes 9296 | tf_op jit(solution)/shard_map/ppermute | solution.py:24
  983.0 71.3 %collective-permute-start.62 = (f32[3,258,1]{1,0,2:T(4,128)}, f32[3,258,1]{1,0,2:T(4,128)}, u32[]{:S(2)}, u32[]{:S(2)}) collective-permute-start(f32[3,258,1]{1,0,2:T(4,128)} %copy.734), channel_id=1, source_target_pairs={{0,1},{1,2},{2,3},{3,4},{4,5},{5,6},{6,7},{7,0},{8,9},{9,10},{10,1... | collective-permute-start | bytes 9296 | tf_op jit(solution)/shard_map/ppermute | solution.py:21
  (106 other events, 1265.4 us)
where the time goes:
time: 1070 us; the launch traced here: 1060 us
  blocking collectives  510 us (48%)
  local copies, waits for them, and re-layouts  218 us (20%)
  starting transfers between devices  135 us (13%)
  other arithmetic  128 us (12%)
  loops' own time  47.1 us (4%)
  waiting for transfers between devices  19.6 us (2%)
    all_gather x1, blocking collectives, shards(): lax.all_gather(turbine_offset, ('gx', 'gy'), axis=0, tiled=True)  303 us
    unnamed x3, blocking collectives  207 us
    ppermute x32, starting transfers between devices, padded_2(): lax.ppermute(lax.slice_in_dim(block, 0, width, axis=dim), axis, backward)  115 us
    gather x36, local copies, waits for them, and re-layouts  49.5 us
    another operation x1, loops' own time, shards(): lax.fori_loop(0, slot_count, add_turbine, jnp.zeros_like(velocity))  47 us
    slice x37, local copies, waits for them, and re-layouts, padded_2(): lax.slice_in_dim(block, block.shape[dim] - width, None, axis=dim)  34.9 us
    sub x6, other arithmetic, advance(): center + advect * (upwind - center)  32.3 us
    slice x22, local copies, waits for them, and re-layouts, padded_2(): lax.slice_in_dim(block, 0, width, axis=dim)  25.5 us
  transfers between devices with their start and end apart: 64, of which 22 were waited for; matrix products, arithmetic and copies ran while one was open for 20% of the time, Pallas kernels for 0%

commit v1 on v0

v1 whole, which is shorter than its diff:
```python
import jax
import jax.numpy as jnp
from jax import lax
from jax.sharding import PartitionSpec as P

LEV = 3
STEPS = 8
FP = 64
MARGIN = 2 * (STEPS - 1)

VERTICAL_MIX = 0.05
DRAG_SCALE = 0.01
HIGHEST = lax.Precision.HIGHEST


def exchange(block, width):
    for axis, dim in (("gx", 1), ("gy", 2)):
        count = lax.axis_size(axis)
        forward = [(i, (i + 1) % count) for i in range(count)]
        backward = [((i + 1) % count, i) for i in range(count)]
        low = lax.ppermute(
            lax.slice_in_dim(block, block.shape[dim] - width, None, axis=dim), axis, forward
        )
        high = lax.ppermute(lax.slice_in_dim(block, 0, width, axis=dim), axis, backward)
        block = jnp.concatenate([low, block, high], axis=dim)
    return block


def drag_law(state):
    return state * jnp.sqrt(state * state + 1.0)


def drag_slope(state):
    square_one = state * state + 1.0
    return (square_one + state * state) / jnp.sqrt(square_one)


def vertical(center):
    zero_row = jnp.zeros_like(center[:1])
    from_above = jnp.concatenate([center[1:] - center[:-1], zero_row], axis=0)
    from_below = jnp.concatenate([zero_row, center[:-1] - center[1:]], axis=0)
    return from_above + from_below


def advance(padded, advect, diffuse, drag_coef):
    center = padded[:, 1:-1, 1:-1]
    upwind = padded[:, :-2, 1:-1]
    downwind = padded[:, 2:, 1:-1]
    left_cell = padded[:, 1:-1, :-2]
    right_cell = padded[:, 1:-1, 2:]
    return (
        center
        + advect * (upwind - center)
        + diffuse * (downwind + upwind + right_cell + left_cell - 4.0 * center)
        + VERTICAL_MIX * vertical(center)
        - drag_coef * drag_law(center)
    )


def retreat(padded, advect_ext, diffuse_ext, drag_coef, state):
    flux_adv = advect_ext * padded
    flux_dif = diffuse_ext * padded
    center = padded[:, 1:-1, 1:-1]
    return (
        center
        - flux_adv[:, 1:-1, 1:-1]
        - 4.0 * flux_dif[:, 1:-1, 1:-1]
        + flux_adv[:, 2:, 1:-1]
        + (
            flux_dif[:, 2:, 1:-1]
            + flux_dif[:, :-2, 1:-1]
            + flux_dif[:, 1:-1, 2:]
            + flux_dif[:, 1:-1, :-2]
        )
        + VERTICAL_MIX * vertical(center)
        - drag_coef * drag_slope(state) * center
    )


def trim(array, margin, wanted):
    excess = margin - wanted
    if excess == 0:
        return array
    return array[:, excess:-excess, excess:-excess]


def profiles(first, starts, widths, period, length):
    pos = (first + jnp.arange(length, dtype=jnp.int32)[None, :] - starts[:, None]) % period
    cell_pos = pos.astype(jnp.float32) - (FP - 1) / 2.0
    profile = jnp.exp(-(cell_pos * cell_pos) / (2.0 * widths[:, None] * widths[:, None]))
    return jnp.where(pos < FP, profile, 0.0)


def level_gain():
    level_pos = jnp.arange(LEV, dtype=jnp.float32) - (LEV - 1) / 2.0
    return DRAG_SCALE * jnp.exp(-0.5 * level_pos * level_pos)


def shards(
    velocity, adjoint_seed, courant, viscosity, turbine_tile, turbine_offset, thrust, disk_width
):
    levels, rows, cols = velocity.shape
    n_gx = lax.axis_size("gx")
    n_gy = lax.axis_size("gy")
    m = MARGIN
    info = jnp.concatenate(
        [
            turbine_tile.astype(jnp.float32),
            turbine_offset.astype(jnp.float32),
            thrust[:, None],
            disk_width[:, None],
        ],
        axis=1,
    )
    info = lax.all_gather(info, ("gx", "gy"), axis=0, tiled=True)
    tiles = info[:, 0].astype(jnp.int32)
    row_start = tiles // n_gy * rows + info[:, 1].astype(jnp.int32)
    col_start = tiles % n_gy * cols + info[:, 2].astype(jnp.int32)
    thrusts = info[:, 3]
    widths = info[:, 4]
    gx = lax.axis_index("gx")
    gy = lax.axis_index("gy")
    prof_r = profiles(gx * rows - m, row_start, widths, n_gx * rows, rows + 2 * m)
    prof_c = profiles(gy * cols - m, col_start, widths, n_gy * cols, cols + 2 * m)
    gain = level_gain()
    plane = jnp.einsum("kr,kc->rc", thrusts[:, None] * prof_r, prof_c, precision=HIGHEST)
    drag = gain[:, None, None] * plane[None]

    ext = exchange(jnp.concatenate([velocity, courant, viscosity, adjoint_seed], axis=0), m)
    advect_all = ext[levels : 2 * levels]
    diffuse_all = ext[2 * levels : 3 * levels]

    state = ext[:levels]
    margin = m
    states = [(state, margin)]
    for _ in range(STEPS - 1):
        margin = margin - 1
        state = advance(
            state, trim(advect_all, m, margin), trim(diffuse_all, m, margin), trim(drag, m, margin)
        )
        states.append((state, margin))

    adjoint = trim(ext[3 * levels :], m, STEPS)
    sensitivity = jnp.zeros_like(velocity)
    for step_index in reversed(range(STEPS)):
        stored, stored_margin = states[step_index]
        sensitivity = sensitivity - trim(adjoint, step_index + 1, 0) * drag_law(
            trim(stored, stored_margin, 0)
        )
        adjoint = retreat(
            adjoint,
            trim(advect_all, m, step_index + 1),
            trim(diffuse_all, m, step_index + 1),
            trim(drag, m, step_index),
            trim(stored, stored_margin, step_index),
        )

    weighted = jnp.einsum("l,lrc->rc", gain, sensitivity, precision=HIGHEST)
    own_r = prof_r[:, m : m + rows]
    own_c = prof_c[:, m : m + cols]
    across = jnp.einsum("rc,kc->kr", weighted, own_c, precision=HIGHEST)
    totals = jnp.sum(own_r * across, axis=1)
    values = thrusts * totals
    grad = lax.psum_scatter(values, ("gx", "gy"), scatter_dimension=0, tiled=True)
    return adjoint, grad


def solution(mesh):
    placed = (
        P(None, "gx", "gy"),
        P(None, "gx", "gy"),
        P(None, "gx", "gy"),
        P(None, "gx", "gy"),
        P(("gx", "gy"), None),
        P(("gx", "gy"), None),
        P(("gx", "gy")),
        P(("gx", "gy")),
    )
    return jax.shard_map(
        shards,
        mesh=mesh,
        in_specs=placed,
        out_specs=(P(None, "gx", "gy"), P(("gx", "gy"))),
        check_vma=False,
    )
```

time: 1070 us -> 469 us (0.44)
  local copies, waits for them, and re-layouts: 218 us -> 18.9 us
  blocking collectives: 510 us -> 383 us
  starting transfers between devices: 135 us -> 8.25 us
  other arithmetic: 128 us -> 47.6 us
  loops' own time: 47.1 us -> 0 us
  waiting for transfers between devices: 19.6 us -> 1.01 us
    unnamed x3 -> x1, blocking collectives: 207 us -> 74.1 us
    ppermute x64 -> x4, starting transfers between devices: 135 us -> 8.25 us  [the longest x2 5.51 us: exchange(): lax.ppermute(lax.slice_in_dim(block, 0, width, axis=dim), axis, backward)]
    gather x41 -> x0, local copies, waits for them, and re-layouts: 53 us -> none
    slice x59 -> x5, local copies, waits for them, and re-layouts: 60.4 us -> 8.38 us  [the longest x3 5.16 us: exchange(): lax.slice_in_dim(block, block.shape[dim] - width, None, axis=dim)]
    another operation x2 -> x0, loops' own time: 47.1 us -> none  [the longest x1 47 us: shards(): lax.fori_loop(0, slot_count, add_turbine, jnp.zeros_like(velocity))]
    ppermute x32 -> x2, local copies, waits for them, and re-layouts: 45.4 us -> 4.54 us  [the longest x1 2.76 us: exchange(): lax.ppermute(lax.slice_in_dim(block, 0, width, axis=dim), axis, backward)]
    sub x6 -> x5, other arithmetic: 32.3 us -> 8.69 us  [advance(): center + advect * (upwind - center)]
    dynamic_update_slice x12 -> x0, local copies, waits for them, and re-layouts: 22.7 us -> none  [add_turbine(): lax.dynamic_update_slice(field_now, block_vals + slot_thrust[slot_index]...]
  transfers between devices with their start and end apart: 64 -> 4, of which waited for: 22 -> 1; matrix products, arithmetic and copies ran while one was open for 20% -> 2% of each run, Pallas kernels for 0% -> 0%
where the time goes in v1:
time: 469 us; the launch traced here: 463 us
  blocking collectives  383 us (82%)
  other arithmetic  47.6 us (10%)
  local copies, waits for them, and re-layouts  18.9 us (4%)
  starting transfers between devices  8.25 us (2%)
    all_gather x1, blocking collectives, shards(): info = lax.all_gather(info, ('gx', 'gy'), axis=0, tiled=True)  309 us
    unnamed x1, blocking collectives  74.1 us
    mul x8, other arithmetic, retreat(): flux_adv = advect_ext * padded  19.6 us
  transfers between devices with their start and end apart: 4, of which 1 were waited for; matrix products, arithmetic and copies ran while one was open for 2% of the time, Pallas kernels for 0%

profile of v1, /device:TPU:1, one launch (start us, length us, event | category | flops | bytes accessed | tf_op | source)
XLA Modules:
  0.0 463.3 jit_solution(9431200315629695435)
XLA Ops:
  0.7 1.0 constant_dynamic-update-slice_fusion.3
  1.7 1.0 constant_dynamic-update-slice_fusion.2
  2.7 1.0 constant_dynamic-update-slice_fusion.1
  3.8 1.0 constant_dynamic-update-slice_fusion
  4.8 0.7 fusion.138
  5.5 2.7 collective-permute-start
  8.3 308.7 %all-gather = f32[128,4,5]{2,1,0:T(4,128)S(1)} all-gather(f32[1,4,5]{2,1,0:T(4,128)S(1)} %bitcast.25), channel_id=1, replica_groups=mesh['gx'=16,'gy'=8] {'gx','gy'}, dimensions={0}, use_global_device_ids=true | all-gather | bytes 10320 | tf_op jit(solution)/shard_map/all_gather | solution.py:115
  317.0 0.3 fusion.139
  317.5 0.1 copy.50
  317.6 0.1 copy.52
  318.0 1.5 fusion.91
  319.5 0.1 broadcast_multiply_fusion
  319.6 1.3 exponential_select_fusion
  320.9 0.2 pad_maximum_fusion.1
  321.1 2.3 fusion.137
  323.4 2.2 copy.34
  325.7 2.9 copy.35
  328.5 5.5 %collective-permute-start.3 = (f32[12,284,14]{1,2,0:T(8,128)}, f32[12,284,14]{1,2,0:T(8,128)}, u32[]{:S(2)}, u32[]{:S(2)}) collective-permute-start(f32[12,284,14]{1,2,0:T(8,128)} %copy.35), channel_id=1, source_target_pairs={{1,0},{2,1},{3,2},{4,3},{5,4},{6,5},{7,6},{0,7},{9,8},{10,9},{11,1... | collective-permute-start | bytes 572552 | tf_op jit(solution)/shard_map/ppermute | solution.py:24
  334.1 1.3 exponential_select_fusion.1
  335.3 1.8 copy.36
  337.1 1.0 collective-permute-done.3
  338.1 2.8 copy.37
  340.9 3.5 pad_maximum_fusion
  344.4 0.4 slice_subtract_fusion.8
  344.7 1.8 fusion.1
  346.5 0.4 slice_subtract_fusion.16
  346.9 1.7 fusion.25
  348.6 0.4 slice_subtract_fusion.14
  348.9 1.7 fusion.19
  350.6 0.4 slice_subtract_fusion.12
  351.0 1.7 fusion.13
  352.7 0.4 slice_subtract_fusion.10
  353.1 1.9 fusion.7
  354.9 0.4 slice_subtract_fusion.24
  355.3 1.8 slice_multiply_fusion.39
  357.1 0.6 slice_subtract_fusion.22
  357.8 3.4 slice_multiply_fusion.37
  361.2 0.3 slice_multiply_fusion.36
  361.5 0.4 slice_subtract_fusion.20
  361.8 2.3 slice_multiply_fusion.15
  364.1 0.3 slice_multiply_fusion.14
  364.4 0.4 slice_subtract_fusion.18
  364.7 2.3 slice_multiply_fusion.11
  367.0 0.3 slice_multiply_fusion.10
  367.3 0.3 slice_subtract_fusion.34
  367.7 2.2 slice_multiply_fusion.33
  369.9 0.3 slice_multiply_fusion.32
  370.2 0.3 slice_subtract_fusion.32
  370.6 2.2 slice_multiply_fusion.29
  372.8 0.5 slice_multiply_fusion.28
  373.3 0.3 slice_subtract_fusion.30
  373.7 2.2 slice_multiply_fusion.25
  375.9 0.3 slice_multiply_fusion.24
  376.2 0.3 slice_subtract_fusion.28
  376.6 3.1 slice_multiply_fusion.21
  379.7 0.3 slice_multiply_fusion.20
  380.0 0.2 slice_subtract_fusion.37
  380.2 0.5 copy-done
  380.8 2.4 fusion.101
  383.2 1.2 fusion.94
  384.3 0.7 fusion
  385.1 74.1 %all-reduce.30 = f32[512]{0:T(512)S(1)} all-reduce(f32[512]{0:T(512)S(1)} %mul.735), channel_id=2, replica_groups=mesh['gx'=16,'gy'=8] {'gx','gy'}, use_global_device_ids=true, to_apply=%region_1.2.clone | all-reduce | flops 512 | bytes 4096
  459.2 0.6 dynamic-slice
  459.8 3.1 fusion.99
  (33 shorter events, 0.7 us)
Async XLA Ops:
  0.6 7.5 %copy-start.4 = (s32[4,2]{0,1:T(2,128)S(1)}, s32[4,2]{0,1:T(2,128)}, u32[]{:S(2)}) copy-start(s32[4,2]{0,1:T(2,128)} %param.13) | copy-start | bytes 100
  0.6 7.5 %copy-start.7 = (s32[4,1]{0,1:T(1,128)S(1)}, s32[4,1]{0,1:T(1,128)}, u32[]{:S(2)}) copy-start(s32[4,1]{0,1:T(1,128)} %param.12) | copy-start | bytes 52
  0.7 7.6 %copy-start.6 = (f32[4]{0:T(128)S(1)}, f32[4]{0:T(128)}, u32[]{:S(2)}) copy-start(f32[4]{0:T(128)} %param.14) | copy-start | bytes 52
  0.7 7.6 %copy-start.5 = (f32[4]{0:T(128)S(1)}, f32[4]{0:T(128)}, u32[]{:S(2)}) copy-start(f32[4]{0:T(128)} %param.15) | copy-start | bytes 52
  5.5 315.4 %collective-permute-start = (f32[12,14,128]{2,1,0:T(8,128)}, f32[12,14,128]{2,1,0:T(8,128)S(1)}, u32[]{:S(2)}, u32[]{:S(2)}) collective-permute-start(f32[12,14,128]{2,1,0:T(8,128)} %get-tuple-element.28), channel_id=1, source_target_pairs={{0,8},{8,16},{16,24},{24,32},{32,40},{40,48},{48,56},{56,64},{64,7... | collective-permute-start | bytes 258056 | tf_op jit(solution)/shard_map/ppermute | solution.py:21
  8.1 312.8 %collective-permute-start.1 = (f32[12,14,128]{2,1,0:T(8,128)S(1)}, f32[12,14,128]{2,1,0:T(8,128)S(1)}, u32[]{:S(2)}, u32[]{:S(2)}) collective-permute-start(f32[12,14,128]{2,1,0:T(8,128)S(1)} %get-tuple-element.29), channel_id=1, source_target_pairs={{8,0},{16,8},{24,16},{32,24},{40,32},{48,40},{56,48},{64,56},{72,6... | collective-permute-start | bytes 258056 | tf_op jit(solution)/shard_map/ppermute | solution.py:24
  325.6 9.7 %collective-permute-start.2 = (f32[12,284,14]{1,2,0:T(8,128)S(1)}, f32[12,284,14]{1,2,0:T(8,128)S(1)}, u32[]{:S(2)}, u32[]{:S(2)}) collective-permute-start(f32[12,284,14]{1,2,0:T(8,128)S(1)} %copy.34), channel_id=1, source_target_pairs={{0,1},{1,2},{2,3},{3,4},{4,5},{5,6},{6,7},{7,0},{8,9},{9,10},{10,1... | collective-permute-start | bytes 572552 | tf_op jit(solution)/shard_map/ppermute | solution.py:21
  328.5 9.6 %collective-permute-start.3 = (f32[12,284,14]{1,2,0:T(8,128)}, f32[12,284,14]{1,2,0:T(8,128)}, u32[]{:S(2)}, u32[]{:S(2)}) collective-permute-start(f32[12,284,14]{1,2,0:T(8,128)} %copy.35), channel_id=1, source_target_pairs={{1,0},{2,1},{3,2},{4,3},{5,4},{6,5},{7,6},{0,7},{9,8},{10,9},{11,1... | collective-permute-start | bytes 572552 | tf_op jit(solution)/shard_map/ppermute | solution.py:24
  379.7 1.0 copy-start
  379.7 1.1 copy-start.1
  380.8 3.5 copy-start.2
  380.8 3.5 copy-start.3
